TPU v7x, 32 devices: a whole 2x2x4 slice. The times are simulated.
32 devices in a mesh: orb: 8 (over y, x, core), slab: 4 (over z).
Axes of the slice: x: 2, y: 2, z: 4, core: 2. Of those that a mesh axis runs over, the one named last changes fastest.
Arguments:
- pool: float32 [16, 32, 32, 128], P('orb', 'slab'), may hold values from -6 to 6
- target_row: int32 [8], P('orb'), may hold values from 0 to 1
- source_index: int32 [3], replicated, may hold values from 0 to 15
- metric: float32 [3, 32, 32, 128], P(None, 'slab'), may hold values from 0.3 to 3
- screening: float32 [32, 32, 128], P('slab'), may hold values from 0.05 to 4
Outputs:
- exchange: float32 [8, 32, 32, 128], P('orb', 'slab')
All inputs are finite; a program needn't handle non-finite values.
Results may differ from a plain program's by a relative error of at most 0.000096.
Values sent between devices are 32-bit elements; how exact they have to be, the bound alone decides.
No kernel may reach another device: no remote copies, remote signals or barrier semaphores. Data moves between devices by JAX's collectives and lax.ppermute only.
A program may use at most 64 MiB of HBM per device.

v0:
```python
import math
import jax
import jax.numpy as jnp
from jax import lax
from jax.sharding import PartitionSpec as P

NSRC = 3
SWEEPS = 6


def extended(cells, sides, width):
    for axis, dim in sides:
        count = lax.axis_size(axis)
        ends = count - 1
        head = lax.slice_in_dim(cells, 0, width, axis=dim)
        tail = lax.slice_in_dim(cells, cells.shape[dim] - width, cells.shape[dim], axis=dim)
        cells = jnp.concatenate(
            [
                lax.ppermute(tail, axis, [(i, (i + 1) % count) for i in range(ends)]),
                cells,
                lax.ppermute(head, axis, [((i + 1) % count, i) for i in range(ends)]),
            ],
            axis=dim,
        )
    return cells


def spread(value, axis, source):
    kept = jnp.where(lax.axis_index(axis) == source, value, 0).astype(value.dtype)
    return lax.psum(kept, axis)


def shifted(array, axis, by):
    size = lax.axis_size(axis)
    pairs = [(i, i + by) for i in range(size) if 0 <= i + by < size]
    return lax.ppermute(array, axis, pairs)


def lower_x(f):
    return jnp.concatenate([jnp.zeros_like(f[..., :1, :]), f[..., :-1, :]], axis=-2)


def upper_x(f):
    return jnp.concatenate([f[..., 1:, :], jnp.zeros_like(f[..., :1, :])], axis=-2)


def lower_y(f):
    return jnp.concatenate([jnp.zeros_like(f[..., :1]), f[..., :-1]], axis=-1)


def upper_y(f):
    return jnp.concatenate([f[..., 1:], jnp.zeros_like(f[..., :1])], axis=-1)


def step_sizes(count):
    return [
        1.0 / (1.025 + 0.975 * math.cos(math.pi * (2 * k + 1) / (2 * count))) for k in range(count)
    ]


def apply_rest(field, up_plane, down_plane, faces, diag):
    face_x, face_y, face_z, below_x, below_y, below_z = faces
    return (
        diag * field
        - face_z * up_plane
        - below_z * down_plane
        - face_x * upper_x(field)
        - below_x * lower_x(field)
        - face_y * upper_y(field)
        - below_y * lower_y(field)
    )


def sweep_rimmed(density, faces, diag, weights):
    field = weights[0] * density / diag
    for k in range(1, SWEEPS):
        padded = extended(field, (("slab", 1),), 1)
        image = apply_rest(field, padded[:, 2:], padded[:, :-2], faces, diag)
        field = field + weights[k] * (density - image) / diag
    return field


def shards(pool, target_row, source_index, metric, screening):
    held = pool.shape[0]
    weights = step_sizes(SWEEPS)
    copies = []
    for s in range(NSRC):
        which = source_index[s]
        mine = lax.dynamic_index_in_dim(pool, which % held, 0, keepdims=False)
        copies.append(spread(mine, "orb", which // held))
    sources = jnp.stack(copies)
    targets = jnp.take(pool, target_row, axis=0)
    face_x, face_y, face_z = (metric[0], metric[1], metric[2])
    last_plane = shifted(face_z[-1:], "slab", 1)
    below_z = jnp.concatenate([last_plane, face_z[:-1]], axis=0)
    below_x, below_y = (lower_x(face_x), lower_y(face_y))
    faces = (face_x, face_y, face_z, below_x, below_y, below_z)
    diag = screening + face_z + below_z + face_x + below_x + face_y + below_y
    density = targets[0][None] * sources
    fields = [sweep_rimmed(density[s : s + 1], faces, diag, weights) for s in range(NSRC)]
    field = jnp.concatenate(fields, axis=0)
    results = [jnp.sum(field * sources, axis=0)]
    return jnp.stack(results)


def solution(mesh):
    in_specs = (
        P("orb", "slab", None, None),
        P("orb"),
        P(),
        P(None, "slab", None, None),
        P("slab", None, None),
    )
    out_specs = P("orb", "slab", None, None)
    return jax.shard_map(shards, mesh=mesh, in_specs=in_specs, out_specs=out_specs, check_vma=False)
```

profile of v0, /device:TPU:24, one launch (start us, length us, event | category | flops | bytes accessed | tf_op | source)
XLA Modules:
  0.0 196.4 jit_solution(3746264836589793208)
XLA Ops:
  6.5 0.7 slice_bitcast_fusion.1
  7.3 1.3 collective-permute-start
  8.6 0.6 fusion.233
  17.2 1.8 fusion.186
  19.1 1.0 copy-done
  20.1 55.9 %all-reduce.65.cloned.1.call-done = (f32[1,8,32,128]{3,2,1,0:T(8,128)}, f32[1,8,32,128]{3,2,1,0:T(8,128)}, f32[1,8,32,128]{3,2,1,0:T(8,128)}) async-done(((f32[1,8,32,128]{3,2,1,0:T(8,128)}, f32[1,8,32,128]{3,2,1,0:T(8,128)}, f32[1,8,32,128]{3,2,1,0:T(8,128)}), (f32[1,8,32,128]{3,2,1,0:T(8,128)}, f32[1,8,32,128]{3,2,1,0:T(8,128)}, f32[1,8,32,128]{3,2,1,0:T(8,128)})) %all-reduce.65.cloned.1.call-update) | async-done | bytes 393232 | tf_op jit(solution)/shard_map/psum | solution.py:30
  76.0 0.9 constant_dynamic-update-slice_fusion.2
  77.0 0.9 copy-done.2
  77.9 0.8 copy-done.1
  78.9 2.4 %collective-permute-start.1 = (f32[1,1,32,128]{3,2,1,0:T(8,128)S(1)}, f32[1,1,32,128]{3,2,1,0:T(8,128)S(1)}, u32[]{:S(2)}, u32[]{:S(2)}) collective-permute-start(f32[1,1,32,128]{3,2,1,0:T(8,128)S(1)} %get-tuple-element.59), channel_id=1, source_target_pairs={{1,0},{2,1},{3,2},{5,4},{6,5},{7,6},{9,8},{10,9},{11,10},{13,12},{... | collective-permute-start | bytes 49160 | tf_op jit(solution)/shard_map/ppermute | solution.py:21
  81.4 1.3 collective-permute-start.2
  82.8 4.2 %collective-permute-done.2 = f32[1,1,32,128]{3,2,1,0:T(8,128)S(1)} collective-permute-done((f32[1,1,32,128]{3,2,1,0:T(8,128)S(1)}, f32[1,1,32,128]{3,2,1,0:T(8,128)S(1)}, u32[]{:S(2)}, u32[]{:S(2)}) %collective-permute-start.2) | collective-permute-done | bytes 16416 | tf_op jit(solution)/shard_map/ppermute | solution.py:19
  87.0 0.2 fusion.178
  87.3 2.4 %collective-permute-start.3 = (f32[1,1,32,128]{3,2,1,0:T(8,128)S(1)}, f32[1,1,32,128]{3,2,1,0:T(8,128)S(1)}, u32[]{:S(2)}, u32[]{:S(2)}) collective-permute-start(f32[1,1,32,128]{3,2,1,0:T(8,128)S(1)} %get-tuple-element.53), channel_id=1, source_target_pairs={{1,0},{2,1},{3,2},{5,4},{6,5},{7,6},{9,8},{10,9},{11,10},{13,12},{... | collective-permute-start | bytes 49160 | tf_op jit(solution)/shard_map/ppermute | solution.py:21
  89.7 1.3 collective-permute-start.4
  91.1 4.2 %collective-permute-done.4 = f32[1,1,32,128]{3,2,1,0:T(8,128)S(1)} collective-permute-done((f32[1,1,32,128]{3,2,1,0:T(8,128)S(1)}, f32[1,1,32,128]{3,2,1,0:T(8,128)S(1)}, u32[]{:S(2)}, u32[]{:S(2)}) %collective-permute-start.4) | collective-permute-done | bytes 16416 | tf_op jit(solution)/shard_map/ppermute | solution.py:19
  95.3 0.2 fusion.166
  95.6 2.5 %collective-permute-start.5 = (f32[1,1,32,128]{3,2,1,0:T(8,128)S(1)}, f32[1,1,32,128]{3,2,1,0:T(8,128)S(1)}, u32[]{:S(2)}, u32[]{:S(2)}) collective-permute-start(f32[1,1,32,128]{3,2,1,0:T(8,128)S(1)} %get-tuple-element.47), channel_id=1, source_target_pairs={{1,0},{2,1},{3,2},{5,4},{6,5},{7,6},{9,8},{10,9},{11,10},{13,12},{... | collective-permute-start | bytes 49160 | tf_op jit(solution)/shard_map/ppermute | solution.py:21
  98.1 1.3 collective-permute-start.6
  99.5 4.2 %collective-permute-done.6 = f32[1,1,32,128]{3,2,1,0:T(8,128)S(1)} collective-permute-done((f32[1,1,32,128]{3,2,1,0:T(8,128)S(1)}, f32[1,1,32,128]{3,2,1,0:T(8,128)S(1)}, u32[]{:S(2)}, u32[]{:S(2)}) %collective-permute-start.6) | collective-permute-done | bytes 16416 | tf_op jit(solution)/shard_map/ppermute | solution.py:19
  103.7 0.2 fusion.154
  104.0 1.9 collective-permute-start.7
  105.9 1.3 collective-permute-start.8
  107.3 4.2 %collective-permute-done.8 = f32[1,1,32,128]{3,2,1,0:T(8,128)S(1)} collective-permute-done((f32[1,1,32,128]{3,2,1,0:T(8,128)S(1)}, f32[1,1,32,128]{3,2,1,0:T(8,128)S(1)}, u32[]{:S(2)}, u32[]{:S(2)}) %collective-permute-start.8) | collective-permute-done | bytes 16416 | tf_op jit(solution)/shard_map/ppermute | solution.py:19
  111.5 0.2 fusion.142
  111.9 1.9 collective-permute-start.11
  113.9 1.3 collective-permute-start.12
  115.2 1.3 collective-permute-start.10
  116.5 5.2 %collective-permute-start.9 = (f32[1,1,32,128]{3,2,1,0:T(8,128)S(1)}, f32[1,1,32,128]{3,2,1,0:T(8,128)S(1)}, u32[]{:S(2)}, u32[]{:S(2)}) collective-permute-start(f32[1,1,32,128]{3,2,1,0:T(8,128)S(1)} %get-tuple-element.35), channel_id=1, source_target_pairs={{1,0},{2,1},{3,2},{5,4},{6,5},{7,6},{9,8},{10,9},{11,10},{13,12},{... | collective-permute-start | bytes 49160 | tf_op jit(solution)/shard_map/ppermute | solution.py:21
  121.7 0.2 fusion.118
  122.1 1.0 collective-permute-done.9
  123.1 0.2 fusion.130
  123.4 4.2 %collective-permute-start.13 = (f32[1,1,32,128]{3,2,1,0:T(8,128)S(1)}, f32[1,1,32,128]{3,2,1,0:T(8,128)S(1)}, u32[]{:S(2)}, u32[]{:S(2)}) collective-permute-start(f32[1,1,32,128]{3,2,1,0:T(8,128)S(1)} %get-tuple-element.83), channel_id=1, source_target_pairs={{1,0},{2,1},{3,2},{5,4},{6,5},{7,6},{9,8},{10,9},{11,10},{13,12},{... | collective-permute-start | bytes 49160 | tf_op jit(solution)/shard_map/ppermute | solution.py:21
  127.6 1.3 collective-permute-start.14
  129.0 4.6 %collective-permute-start.21 = (f32[1,1,32,128]{3,2,1,0:T(8,128)S(1)}, f32[1,1,32,128]{3,2,1,0:T(8,128)S(1)}, u32[]{:S(2)}, u32[]{:S(2)}) collective-permute-start(f32[1,1,32,128]{3,2,1,0:T(8,128)S(1)} %get-tuple-element.119), channel_id=1, source_target_pairs={{1,0},{2,1},{3,2},{5,4},{6,5},{7,6},{9,8},{10,9},{11,10},{13,12},{... | collective-permute-start | bytes 49160 | tf_op jit(solution)/shard_map/ppermute | solution.py:21
  133.5 1.3 collective-permute-start.22
  134.8 0.2 fusion.106
  135.2 3.9 %collective-permute-done.22 = f32[1,1,32,128]{3,2,1,0:T(8,128)S(1)} collective-permute-done((f32[1,1,32,128]{3,2,1,0:T(8,128)S(1)}, f32[1,1,32,128]{3,2,1,0:T(8,128)S(1)}, u32[]{:S(2)}, u32[]{:S(2)}) %collective-permute-start.22) | collective-permute-done | bytes 16416 | tf_op jit(solution)/shard_map/ppermute | solution.py:19
  139.1 0.2 fusion.58
  139.5 3.9 %collective-permute-start.15 = (f32[1,1,32,128]{3,2,1,0:T(8,128)S(1)}, f32[1,1,32,128]{3,2,1,0:T(8,128)S(1)}, u32[]{:S(2)}, u32[]{:S(2)}) collective-permute-start(f32[1,1,32,128]{3,2,1,0:T(8,128)S(1)} %get-tuple-element.77), channel_id=1, source_target_pairs={{1,0},{2,1},{3,2},{5,4},{6,5},{7,6},{9,8},{10,9},{11,10},{13,12},{... | collective-permute-start | bytes 49160 | tf_op jit(solution)/shard_map/ppermute | solution.py:21
  143.4 1.3 collective-permute-start.16
  144.7 4.5 %collective-permute-start.23 = (f32[1,1,32,128]{3,2,1,0:T(8,128)S(1)}, f32[1,1,32,128]{3,2,1,0:T(8,128)S(1)}, u32[]{:S(2)}, u32[]{:S(2)}) collective-permute-start(f32[1,1,32,128]{3,2,1,0:T(8,128)S(1)} %get-tuple-element.113), channel_id=1, source_target_pairs={{1,0},{2,1},{3,2},{5,4},{6,5},{7,6},{9,8},{10,9},{11,10},{13,12},{... | collective-permute-start | bytes 49160 | tf_op jit(solution)/shard_map/ppermute | solution.py:21
  149.3 1.3 collective-permute-start.24
  150.6 0.2 fusion.94
  151.0 3.9 %collective-permute-done.24 = f32[1,1,32,128]{3,2,1,0:T(8,128)S(1)} collective-permute-done((f32[1,1,32,128]{3,2,1,0:T(8,128)S(1)}, f32[1,1,32,128]{3,2,1,0:T(8,128)S(1)}, u32[]{:S(2)}, u32[]{:S(2)}) %collective-permute-start.24) | collective-permute-done | bytes 16416 | tf_op jit(solution)/shard_map/ppermute | solution.py:19
  154.9 0.2 fusion.46
  155.3 1.9 collective-permute-start.17
  157.2 1.3 collective-permute-start.18
  158.5 4.5 %collective-permute-start.25 = (f32[1,1,32,128]{3,2,1,0:T(8,128)S(1)}, f32[1,1,32,128]{3,2,1,0:T(8,128)S(1)}, u32[]{:S(2)}, u32[]{:S(2)}) collective-permute-start(f32[1,1,32,128]{3,2,1,0:T(8,128)S(1)} %get-tuple-element.107), channel_id=1, source_target_pairs={{1,0},{2,1},{3,2},{5,4},{6,5},{7,6},{9,8},{10,9},{11,10},{13,12},{... | collective-permute-start | bytes 49160 | tf_op jit(solution)/shard_map/ppermute | solution.py:21
  163.1 1.3 collective-permute-start.26
  164.4 0.2 fusion.82
  164.7 4.0 %collective-permute-done.26 = f32[1,1,32,128]{3,2,1,0:T(8,128)S(1)} collective-permute-done((f32[1,1,32,128]{3,2,1,0:T(8,128)S(1)}, f32[1,1,32,128]{3,2,1,0:T(8,128)S(1)}, u32[]{:S(2)}, u32[]{:S(2)}) %collective-permute-start.26) | collective-permute-done | bytes 16416 | tf_op jit(solution)/shard_map/ppermute | solution.py:19
  168.7 0.2 fusion.34
  169.0 1.9 collective-permute-start.27
  171.0 1.3 collective-permute-start.28
  172.3 4.5 %collective-permute-start.19 = (f32[1,1,32,128]{3,2,1,0:T(8,128)S(1)}, f32[1,1,32,128]{3,2,1,0:T(8,128)S(1)}, u32[]{:S(2)}, u32[]{:S(2)}) collective-permute-start(f32[1,1,32,128]{3,2,1,0:T(8,128)S(1)} %get-tuple-element.65), channel_id=1, source_target_pairs={{1,0},{2,1},{3,2},{5,4},{6,5},{7,6},{9,8},{10,9},{11,10},{13,12},{... | collective-permute-start | bytes 49160 | tf_op jit(solution)/shard_map/ppermute | solution.py:21
  176.8 1.3 collective-permute-start.20
  178.2 0.2 fusion.22
  178.4 4.5 %collective-permute-start.29 = (f32[1,1,32,128]{3,2,1,0:T(8,128)S(1)}, f32[1,1,32,128]{3,2,1,0:T(8,128)S(1)}, u32[]{:S(2)}, u32[]{:S(2)}) collective-permute-start(f32[1,1,32,128]{3,2,1,0:T(8,128)S(1)} %get-tuple-element.95), channel_id=1, source_target_pairs={{1,0},{2,1},{3,2},{5,4},{6,5},{7,6},{9,8},{10,9},{11,10},{13,12},{... | collective-permute-start | bytes 49160 | tf_op jit(solution)/shard_map/ppermute | solution.py:21
  183.0 1.3 collective-permute-start.30
  184.3 0.2 fusion.70
  184.6 4.0 %collective-permute-done.30 = f32[1,1,32,128]{3,2,1,0:T(8,128)S(1)} collective-permute-done((f32[1,1,32,128]{3,2,1,0:T(8,128)S(1)}, f32[1,1,32,128]{3,2,1,0:T(8,128)S(1)}, u32[]{:S(2)}, u32[]{:S(2)}) %collective-permute-start.30) | collective-permute-done | bytes 16416 | tf_op jit(solution)/shard_map/ppermute | solution.py:19
  188.6 0.2 fusion.10
  188.8 0.7 fusion
  (80 shorter events, 2.1 us)
Async XLA Ops:
  6.5 69.4 %all-reduce.65.cloned.1.call-start = ((), (), s32[]{:S(2)}) async-start(), calls=%async_computation | async-start | bytes 786432 | tf_op jit(solution)/shard_map/psum | solution.py:30
  6.5 2.0 %copy-start.4 = (s32[3]{0:T(128)S(1)}, s32[3]{0:T(128)}, u32[]{:S(2)}) copy-start(s32[3]{0:T(128)} %param.7) | copy-start | bytes 40
  7.3 70.6 %collective-permute-start = (f32[1,32,128]{2,1,0:T(8,128)S(1)}, f32[1,32,128]{2,1,0:T(8,128)S(1)}, u32[]{:S(2)}, u32[]{:S(2)}) collective-permute-start(f32[1,32,128]{2,1,0:T(8,128)S(1)} %slice_bitcast_fusion.1), channel_id=1, source_target_pairs={{0,1},{1,2},{2,3},{4,5},{5,6},{6,7},{8,9},{9,10},{10,11},{12,13},{... | collective-permute-start | bytes 49160 | tf_op jit(solution)/shard_map/ppermute | solution.py:36
  19.0 1.0 copy-start
  76.0 1.0 copy-start.3
  76.9 0.9 copy-start.2
  77.9 0.9 copy-start.1
  78.9 3.9 %collective-permute-start.1 = (f32[1,1,32,128]{3,2,1,0:T(8,128)S(1)}, f32[1,1,32,128]{3,2,1,0:T(8,128)S(1)}, u32[]{:S(2)}, u32[]{:S(2)}) collective-permute-start(f32[1,1,32,128]{3,2,1,0:T(8,128)S(1)} %get-tuple-element.59), channel_id=1, source_target_pairs={{1,0},{2,1},{3,2},{5,4},{6,5},{7,6},{9,8},{10,9},{11,10},{13,12},{... | collective-permute-start | bytes 49160 | tf_op jit(solution)/shard_map/ppermute | solution.py:21
  81.4 5.6 %collective-permute-start.2 = (f32[1,1,32,128]{3,2,1,0:T(8,128)S(1)}, f32[1,1,32,128]{3,2,1,0:T(8,128)S(1)}, u32[]{:S(2)}, u32[]{:S(2)}) collective-permute-start(f32[1,1,32,128]{3,2,1,0:T(8,128)S(1)} %get-tuple-element.60), channel_id=1, source_target_pairs={{0,1},{1,2},{2,3},{4,5},{5,6},{6,7},{8,9},{9,10},{10,11},{12,13},{... | collective-permute-start | bytes 49160 | tf_op jit(solution)/shard_map/ppermute | solution.py:19
  87.3 3.9 %collective-permute-start.3 = (f32[1,1,32,128]{3,2,1,0:T(8,128)S(1)}, f32[1,1,32,128]{3,2,1,0:T(8,128)S(1)}, u32[]{:S(2)}, u32[]{:S(2)}) collective-permute-start(f32[1,1,32,128]{3,2,1,0:T(8,128)S(1)} %get-tuple-element.53), channel_id=1, source_target_pairs={{1,0},{2,1},{3,2},{5,4},{6,5},{7,6},{9,8},{10,9},{11,10},{13,12},{... | collective-permute-start | bytes 49160 | tf_op jit(solution)/shard_map/ppermute | solution.py:21
  89.7 5.6 %collective-permute-start.4 = (f32[1,1,32,128]{3,2,1,0:T(8,128)S(1)}, f32[1,1,32,128]{3,2,1,0:T(8,128)S(1)}, u32[]{:S(2)}, u32[]{:S(2)}) collective-permute-start(f32[1,1,32,128]{3,2,1,0:T(8,128)S(1)} %get-tuple-element.54), channel_id=1, source_target_pairs={{0,1},{1,2},{2,3},{4,5},{5,6},{6,7},{8,9},{9,10},{10,11},{12,13},{... | collective-permute-start | bytes 49160 | tf_op jit(solution)/shard_map/ppermute | solution.py:19
  95.6 3.9 %collective-permute-start.5 = (f32[1,1,32,128]{3,2,1,0:T(8,128)S(1)}, f32[1,1,32,128]{3,2,1,0:T(8,128)S(1)}, u32[]{:S(2)}, u32[]{:S(2)}) collective-permute-start(f32[1,1,32,128]{3,2,1,0:T(8,128)S(1)} %get-tuple-element.47), channel_id=1, source_target_pairs={{1,0},{2,1},{3,2},{5,4},{6,5},{7,6},{9,8},{10,9},{11,10},{13,12},{... | collective-permute-start | bytes 49160 | tf_op jit(solution)/shard_map/ppermute | solution.py:21
  98.1 5.6 %collective-permute-start.6 = (f32[1,1,32,128]{3,2,1,0:T(8,128)S(1)}, f32[1,1,32,128]{3,2,1,0:T(8,128)S(1)}, u32[]{:S(2)}, u32[]{:S(2)}) collective-permute-start(f32[1,1,32,128]{3,2,1,0:T(8,128)S(1)} %get-tuple-element.48), channel_id=1, source_target_pairs={{0,1},{1,2},{2,3},{4,5},{5,6},{6,7},{8,9},{9,10},{10,11},{12,13},{... | collective-permute-start | bytes 49160 | tf_op jit(solution)/shard_map/ppermute | solution.py:19
  104.0 3.4 %collective-permute-start.7 = (f32[1,1,32,128]{3,2,1,0:T(8,128)S(1)}, f32[1,1,32,128]{3,2,1,0:T(8,128)S(1)}, u32[]{:S(2)}, u32[]{:S(2)}) collective-permute-start(f32[1,1,32,128]{3,2,1,0:T(8,128)S(1)} %get-tuple-element.41), channel_id=1, source_target_pairs={{1,0},{2,1},{3,2},{5,4},{6,5},{7,6},{9,8},{10,9},{11,10},{13,12},{... | collective-permute-start | bytes 49160 | tf_op jit(solution)/shard_map/ppermute | solution.py:21
  105.9 5.6 %collective-permute-start.8 = (f32[1,1,32,128]{3,2,1,0:T(8,128)S(1)}, f32[1,1,32,128]{3,2,1,0:T(8,128)S(1)}, u32[]{:S(2)}, u32[]{:S(2)}) collective-permute-start(f32[1,1,32,128]{3,2,1,0:T(8,128)S(1)} %get-tuple-element.42), channel_id=1, source_target_pairs={{0,1},{1,2},{2,3},{4,5},{5,6},{6,7},{8,9},{9,10},{10,11},{12,13},{... | collective-permute-start | bytes 49160 | tf_op jit(solution)/shard_map/ppermute | solution.py:19
  111.9 9.7 %collective-permute-start.11 = (f32[1,1,32,128]{3,2,1,0:T(8,128)S(1)}, f32[1,1,32,128]{3,2,1,0:T(8,128)S(1)}, u32[]{:S(2)}, u32[]{:S(2)}) collective-permute-start(f32[1,1,32,128]{3,2,1,0:T(8,128)S(1)} %get-tuple-element.89), channel_id=1, source_target_pairs={{1,0},{2,1},{3,2},{5,4},{6,5},{7,6},{9,8},{10,9},{11,10},{13,12},{... | collective-permute-start | bytes 49160 | tf_op jit(solution)/shard_map/ppermute | solution.py:21
  113.9 7.8 %collective-permute-start.12 = (f32[1,1,32,128]{3,2,1,0:T(8,128)S(1)}, f32[1,1,32,128]{3,2,1,0:T(8,128)S(1)}, u32[]{:S(2)}, u32[]{:S(2)}) collective-permute-start(f32[1,1,32,128]{3,2,1,0:T(8,128)S(1)} %get-tuple-element.90), channel_id=1, source_target_pairs={{0,1},{1,2},{2,3},{4,5},{5,6},{6,7},{8,9},{9,10},{10,11},{12,13},{... | collective-permute-start | bytes 49160 | tf_op jit(solution)/shard_map/ppermute | solution.py:19
  115.2 6.9 %collective-permute-start.10 = (f32[1,1,32,128]{3,2,1,0:T(8,128)S(1)}, f32[1,1,32,128]{3,2,1,0:T(8,128)S(1)}, u32[]{:S(2)}, u32[]{:S(2)}) collective-permute-start(f32[1,1,32,128]{3,2,1,0:T(8,128)S(1)} %get-tuple-element.36), channel_id=1, source_target_pairs={{0,1},{1,2},{2,3},{4,5},{5,6},{6,7},{8,9},{9,10},{10,11},{12,13},{... | collective-permute-start | bytes 49160 | tf_op jit(solution)/shard_map/ppermute | solution.py:19
  116.5 6.6 %collective-permute-start.9 = (f32[1,1,32,128]{3,2,1,0:T(8,128)S(1)}, f32[1,1,32,128]{3,2,1,0:T(8,128)S(1)}, u32[]{:S(2)}, u32[]{:S(2)}) collective-permute-start(f32[1,1,32,128]{3,2,1,0:T(8,128)S(1)} %get-tuple-element.35), channel_id=1, source_target_pairs={{1,0},{2,1},{3,2},{5,4},{6,5},{7,6},{9,8},{10,9},{11,10},{13,12},{... | collective-permute-start | bytes 49160 | tf_op jit(solution)/shard_map/ppermute | solution.py:21
  123.4 11.4 %collective-permute-start.13 = (f32[1,1,32,128]{3,2,1,0:T(8,128)S(1)}, f32[1,1,32,128]{3,2,1,0:T(8,128)S(1)}, u32[]{:S(2)}, u32[]{:S(2)}) collective-permute-start(f32[1,1,32,128]{3,2,1,0:T(8,128)S(1)} %get-tuple-element.83), channel_id=1, source_target_pairs={{1,0},{2,1},{3,2},{5,4},{6,5},{7,6},{9,8},{10,9},{11,10},{13,12},{... | collective-permute-start | bytes 49160 | tf_op jit(solution)/shard_map/ppermute | solution.py:21
  127.6 7.2 %collective-permute-start.14 = (f32[1,1,32,128]{3,2,1,0:T(8,128)S(1)}, f32[1,1,32,128]{3,2,1,0:T(8,128)S(1)}, u32[]{:S(2)}, u32[]{:S(2)}) collective-permute-start(f32[1,1,32,128]{3,2,1,0:T(8,128)S(1)} %get-tuple-element.84), channel_id=1, source_target_pairs={{0,1},{1,2},{2,3},{4,5},{5,6},{6,7},{8,9},{9,10},{10,11},{12,13},{... | collective-permute-start | bytes 49160 | tf_op jit(solution)/shard_map/ppermute | solution.py:19
  129.0 6.2 %collective-permute-start.21 = (f32[1,1,32,128]{3,2,1,0:T(8,128)S(1)}, f32[1,1,32,128]{3,2,1,0:T(8,128)S(1)}, u32[]{:S(2)}, u32[]{:S(2)}) collective-permute-start(f32[1,1,32,128]{3,2,1,0:T(8,128)S(1)} %get-tuple-element.119), channel_id=1, source_target_pairs={{1,0},{2,1},{3,2},{5,4},{6,5},{7,6},{9,8},{10,9},{11,10},{13,12},{... | collective-permute-start | bytes 49160 | tf_op jit(solution)/shard_map/ppermute | solution.py:21
  133.5 5.6 %collective-permute-start.22 = (f32[1,1,32,128]{3,2,1,0:T(8,128)S(1)}, f32[1,1,32,128]{3,2,1,0:T(8,128)S(1)}, u32[]{:S(2)}, u32[]{:S(2)}) collective-permute-start(f32[1,1,32,128]{3,2,1,0:T(8,128)S(1)} %get-tuple-element.120), channel_id=1, source_target_pairs={{0,1},{1,2},{2,3},{4,5},{5,6},{6,7},{8,9},{9,10},{10,11},{12,13},{... | collective-permute-start | bytes 49160 | tf_op jit(solution)/shard_map/ppermute | solution.py:19
  139.5 11.1 %collective-permute-start.15 = (f32[1,1,32,128]{3,2,1,0:T(8,128)S(1)}, f32[1,1,32,128]{3,2,1,0:T(8,128)S(1)}, u32[]{:S(2)}, u32[]{:S(2)}) collective-permute-start(f32[1,1,32,128]{3,2,1,0:T(8,128)S(1)} %get-tuple-element.77), channel_id=1, source_target_pairs={{1,0},{2,1},{3,2},{5,4},{6,5},{7,6},{9,8},{10,9},{11,10},{13,12},{... | collective-permute-start | bytes 49160 | tf_op jit(solution)/shard_map/ppermute | solution.py:21
  143.4 7.2 %collective-permute-start.16 = (f32[1,1,32,128]{3,2,1,0:T(8,128)S(1)}, f32[1,1,32,128]{3,2,1,0:T(8,128)S(1)}, u32[]{:S(2)}, u32[]{:S(2)}) collective-permute-start(f32[1,1,32,128]{3,2,1,0:T(8,128)S(1)} %get-tuple-element.78), channel_id=1, source_target_pairs={{0,1},{1,2},{2,3},{4,5},{5,6},{6,7},{8,9},{9,10},{10,11},{12,13},{... | collective-permute-start | bytes 49160 | tf_op jit(solution)/shard_map/ppermute | solution.py:19
  144.7 6.2 %collective-permute-start.23 = (f32[1,1,32,128]{3,2,1,0:T(8,128)S(1)}, f32[1,1,32,128]{3,2,1,0:T(8,128)S(1)}, u32[]{:S(2)}, u32[]{:S(2)}) collective-permute-start(f32[1,1,32,128]{3,2,1,0:T(8,128)S(1)} %get-tuple-element.113), channel_id=1, source_target_pairs={{1,0},{2,1},{3,2},{5,4},{6,5},{7,6},{9,8},{10,9},{11,10},{13,12},{... | collective-permute-start | bytes 49160 | tf_op jit(solution)/shard_map/ppermute | solution.py:21
  149.3 5.6 %collective-permute-start.24 = (f32[1,1,32,128]{3,2,1,0:T(8,128)S(1)}, f32[1,1,32,128]{3,2,1,0:T(8,128)S(1)}, u32[]{:S(2)}, u32[]{:S(2)}) collective-permute-start(f32[1,1,32,128]{3,2,1,0:T(8,128)S(1)} %get-tuple-element.114), channel_id=1, source_target_pairs={{0,1},{1,2},{2,3},{4,5},{5,6},{6,7},{8,9},{9,10},{10,11},{12,13},{... | collective-permute-start | bytes 49160 | tf_op jit(solution)/shard_map/ppermute | solution.py:19
  155.3 9.1 %collective-permute-start.17 = (f32[1,1,32,128]{3,2,1,0:T(8,128)S(1)}, f32[1,1,32,128]{3,2,1,0:T(8,128)S(1)}, u32[]{:S(2)}, u32[]{:S(2)}) collective-permute-start(f32[1,1,32,128]{3,2,1,0:T(8,128)S(1)} %get-tuple-element.71), channel_id=1, source_target_pairs={{1,0},{2,1},{3,2},{5,4},{6,5},{7,6},{9,8},{10,9},{11,10},{13,12},{... | collective-permute-start | bytes 49160 | tf_op jit(solution)/shard_map/ppermute | solution.py:21
  157.2 7.2 %collective-permute-start.18 = (f32[1,1,32,128]{3,2,1,0:T(8,128)S(1)}, f32[1,1,32,128]{3,2,1,0:T(8,128)S(1)}, u32[]{:S(2)}, u32[]{:S(2)}) collective-permute-start(f32[1,1,32,128]{3,2,1,0:T(8,128)S(1)} %get-tuple-element.72), channel_id=1, source_target_pairs={{0,1},{1,2},{2,3},{4,5},{5,6},{6,7},{8,9},{9,10},{10,11},{12,13},{... | collective-permute-start | bytes 49160 | tf_op jit(solution)/shard_map/ppermute | solution.py:19
  158.5 6.2 %collective-permute-start.25 = (f32[1,1,32,128]{3,2,1,0:T(8,128)S(1)}, f32[1,1,32,128]{3,2,1,0:T(8,128)S(1)}, u32[]{:S(2)}, u32[]{:S(2)}) collective-permute-start(f32[1,1,32,128]{3,2,1,0:T(8,128)S(1)} %get-tuple-element.107), channel_id=1, source_target_pairs={{1,0},{2,1},{3,2},{5,4},{6,5},{7,6},{9,8},{10,9},{11,10},{13,12},{... | collective-permute-start | bytes 49160 | tf_op jit(solution)/shard_map/ppermute | solution.py:21
  163.1 5.6 %collective-permute-start.26 = (f32[1,1,32,128]{3,2,1,0:T(8,128)S(1)}, f32[1,1,32,128]{3,2,1,0:T(8,128)S(1)}, u32[]{:S(2)}, u32[]{:S(2)}) collective-permute-start(f32[1,1,32,128]{3,2,1,0:T(8,128)S(1)} %get-tuple-element.108), channel_id=1, source_target_pairs={{0,1},{1,2},{2,3},{4,5},{5,6},{6,7},{8,9},{9,10},{10,11},{12,13},{... | collective-permute-start | bytes 49160 | tf_op jit(solution)/shard_map/ppermute | solution.py:19
  169.0 9.1 %collective-permute-start.27 = (f32[1,1,32,128]{3,2,1,0:T(8,128)S(1)}, f32[1,1,32,128]{3,2,1,0:T(8,128)S(1)}, u32[]{:S(2)}, u32[]{:S(2)}) collective-permute-start(f32[1,1,32,128]{3,2,1,0:T(8,128)S(1)} %get-tuple-element.101), channel_id=1, source_target_pairs={{1,0},{2,1},{3,2},{5,4},{6,5},{7,6},{9,8},{10,9},{11,10},{13,12},{... | collective-permute-start | bytes 49160 | tf_op jit(solution)/shard_map/ppermute | solution.py:21
  171.0 7.2 %collective-permute-start.28 = (f32[1,1,32,128]{3,2,1,0:T(8,128)S(1)}, f32[1,1,32,128]{3,2,1,0:T(8,128)S(1)}, u32[]{:S(2)}, u32[]{:S(2)}) collective-permute-start(f32[1,1,32,128]{3,2,1,0:T(8,128)S(1)} %get-tuple-element.102), channel_id=1, source_target_pairs={{0,1},{1,2},{2,3},{4,5},{5,6},{6,7},{8,9},{9,10},{10,11},{12,13},{... | collective-permute-start | bytes 49160 | tf_op jit(solution)/shard_map/ppermute | solution.py:19
  172.3 12.0 %collective-permute-start.19 = (f32[1,1,32,128]{3,2,1,0:T(8,128)S(1)}, f32[1,1,32,128]{3,2,1,0:T(8,128)S(1)}, u32[]{:S(2)}, u32[]{:S(2)}) collective-permute-start(f32[1,1,32,128]{3,2,1,0:T(8,128)S(1)} %get-tuple-element.65), channel_id=1, source_target_pairs={{1,0},{2,1},{3,2},{5,4},{6,5},{7,6},{9,8},{10,9},{11,10},{13,12},{... | collective-permute-start | bytes 49160 | tf_op jit(solution)/shard_map/ppermute | solution.py:21
  176.8 7.5 %collective-permute-start.20 = (f32[1,1,32,128]{3,2,1,0:T(8,128)S(1)}, f32[1,1,32,128]{3,2,1,0:T(8,128)S(1)}, u32[]{:S(2)}, u32[]{:S(2)}) collective-permute-start(f32[1,1,32,128]{3,2,1,0:T(8,128)S(1)} %get-tuple-element.66), channel_id=1, source_target_pairs={{0,1},{1,2},{2,3},{4,5},{5,6},{6,7},{8,9},{9,10},{10,11},{12,13},{... | collective-permute-start | bytes 49160 | tf_op jit(solution)/shard_map/ppermute | solution.py:19
  178.4 6.2 %collective-permute-start.29 = (f32[1,1,32,128]{3,2,1,0:T(8,128)S(1)}, f32[1,1,32,128]{3,2,1,0:T(8,128)S(1)}, u32[]{:S(2)}, u32[]{:S(2)}) collective-permute-start(f32[1,1,32,128]{3,2,1,0:T(8,128)S(1)} %get-tuple-element.95), channel_id=1, source_target_pairs={{1,0},{2,1},{3,2},{5,4},{6,5},{7,6},{9,8},{10,9},{11,10},{13,12},{... | collective-permute-start | bytes 49160 | tf_op jit(solution)/shard_map/ppermute | solution.py:21
  183.0 5.6 %collective-permute-start.30 = (f32[1,1,32,128]{3,2,1,0:T(8,128)S(1)}, f32[1,1,32,128]{3,2,1,0:T(8,128)S(1)}, u32[]{:S(2)}, u32[]{:S(2)}) collective-permute-start(f32[1,1,32,128]{3,2,1,0:T(8,128)S(1)} %get-tuple-element.96), channel_id=1, source_target_pairs={{0,1},{1,2},{2,3},{4,5},{5,6},{6,7},{8,9},{9,10},{10,11},{12,13},{... | collective-permute-start | bytes 49160 | tf_op jit(solution)/shard_map/ppermute | solution.py:19
Sparse Core Ops, SparseCore 0:
  19.2 56.7 all-reduce.64
where the time goes:
time: 198 us; the launch traced here: 196 us
  waiting for transfers between devices  89.7 us (45%)
  starting transfers between devices  71.7 us (36%)
  between operations  22.2 us (11%)
  local copies, waits for them, and re-layouts  6.69 us (3%)
  other arithmetic  5.98 us (3%)
    psum x1, waiting for transfers between devices, spread(): return lax.psum(kept, axis)  55.9 us
    ppermute x15, starting transfers between devices, extended(): lax.ppermute(head, axis, [((i + 1) % count, i) for i in range(ends)])  51.1 us
    ppermute x15, waiting for transfers between devices, extended(): lax.ppermute(tail, axis, [(i, (i + 1) % count) for i in range(ends)])  32.7 us
    ppermute x15, starting transfers between devices, extended(): lax.ppermute(tail, axis, [(i, (i + 1) % count) for i in range(ends)])  19.4 us
  transfers between devices with their start and end apart: 32, of which 10 were waited for; matrix products, arithmetic and copies ran while one was open for 3% of the time, Pallas kernels for 0%

commit v1 on v0

--- a/solution.py
+++ b/solution.py
@@ -27,7 +27,7 @@
 
 def spread(value, axis, source):
     kept = jnp.where(lax.axis_index(axis) == source, value, 0).astype(value.dtype)
-    return lax.psum(kept, axis)
+    return jnp.sum(lax.all_gather(kept, axis), axis=0)
 
 
 def shifted(array, axis, by):

time: 198 us -> 214 us (1.081)
  waiting for transfers between devices: 89.7 us -> 105 us
  other arithmetic: 5.98 us -> 9.91 us
  local copies, waits for them, and re-layouts: 6.69 us -> 3.92 us
    all_gather x0 -> x3, waiting for transfers between devices: none -> 70 us  [spread(): return jnp.sum(lax.all_gather(kept, axis), axis=0)]
    psum x1 -> x0, waiting for transfers between devices: 55.9 us -> none  [spread(): return lax.psum(kept, axis)]
    reduce_sum x0 -> x3, other arithmetic: none -> 3.92 us  [spread(): return jnp.sum(lax.all_gather(kept, axis), axis=0)]
    unnamed x12 -> x4, local copies, waits for them, and re-layouts: 3.67 us -> 0.85 us
  transfers between devices with their start and end apart: 32 -> 34, of which waited for: 10 -> 12; matrix products, arithmetic and copies ran while one was open for 3% -> 3% of each run, Pallas kernels for 0% -> 0%
where the time goes in v1:
time: 214 us; the launch traced here: 213 us
  waiting for transfers between devices  105 us (49%)
  starting transfers between devices  71.6 us (33%)
  between operations  22.2 us (10%)
  other arithmetic  9.91 us (5%)
  local copies, waits for them, and re-layouts  3.92 us (2%)
    all_gather x3, waiting for transfers between devices, spread(): return jnp.sum(lax.all_gather(kept, axis), axis=0)  70 us
    ppermute x15, starting transfers between devices, extended(): lax.ppermute(head, axis, [((i + 1) % count, i) for i in range(ends)])  50.8 us
    ppermute x15, waiting for transfers between devices, extended(): lax.ppermute(tail, axis, [(i, (i + 1) % count) for i in range(ends)])  32.9 us
    ppermute x15, starting transfers between devices, extended(): lax.ppermute(tail, axis, [(i, (i + 1) % count) for i in range(ends)])  19.4 us
  transfers between devices with their start and end apart: 34, of which 12 were waited for; matrix products, arithmetic and copies ran while one was open for 3% of the time, Pallas kernels for 0%

profile of v1, /device:TPU:24, one launch (start us, length us, event | category | flops | bytes accessed | tf_op | source)
XLA Modules:
  0.0 213.1 jit_solution(18259972495252376488)
XLA Ops:
  6.5 1.4 fusion.234
  16.3 1.9 fusion.187
  18.2 0.7 all-gather.6.cloned.1.call-update
  18.9 0.7 all-gather.8.cloned.1.call-update
  19.7 1.3 collective-permute-start
  21.0 21.8 %all-gather.4.cloned.1.call-done = f32[8,8,32,128]{3,2,1,0:T(8,128)} async-done(((f32[1,8,32,128]{3,2,1,0:T(8,128)}), f32[8,8,32,128]{3,2,1,0:T(8,128)}) %all-gather.4.cloned.1.call-update) | async-done | bytes 1048592 | tf_op jit(solution)/shard_map/all_gather | solution.py:30
  42.8 1.3 reduce_sum.36
  44.1 24.1 %all-gather.6.cloned.1.call-done = f32[8,8,32,128]{3,2,1,0:T(8,128)} async-done(((f32[1,8,32,128]{3,2,1,0:T(8,128)}), f32[8,8,32,128]{3,2,1,0:T(8,128)}) %all-gather.6.cloned.1.call-update) | async-done | bytes 1048592 | tf_op jit(solution)/shard_map/all_gather | solution.py:30
  68.2 1.3 reduce_sum.37
  69.5 24.1 %all-gather.8.cloned.1.call-done = f32[8,8,32,128]{3,2,1,0:T(8,128)} async-done(((f32[1,8,32,128]{3,2,1,0:T(8,128)}), f32[8,8,32,128]{3,2,1,0:T(8,128)}) %all-gather.8.cloned.1.call-update) | async-done | bytes 1048592 | tf_op jit(solution)/shard_map/all_gather | solution.py:30
  93.6 1.3 reduce_sum.38
  95.0 0.8 copy-done.1
  96.0 2.4 %collective-permute-start.1 = (f32[1,1,32,128]{3,2,1,0:T(8,128)S(1)}, f32[1,1,32,128]{3,2,1,0:T(8,128)S(1)}, u32[]{:S(2)}, u32[]{:S(2)}) collective-permute-start(f32[1,1,32,128]{3,2,1,0:T(8,128)S(1)} %get-tuple-element.56), channel_id=1, source_target_pairs={{1,0},{2,1},{3,2},{5,4},{6,5},{7,6},{9,8},{10,9},{11,10},{13,12},{... | collective-permute-start | bytes 49160 | tf_op jit(solution)/shard_map/ppermute | solution.py:21
  98.4 1.3 collective-permute-start.2
  99.8 4.2 %collective-permute-done.2 = f32[1,1,32,128]{3,2,1,0:T(8,128)S(1)} collective-permute-done((f32[1,1,32,128]{3,2,1,0:T(8,128)S(1)}, f32[1,1,32,128]{3,2,1,0:T(8,128)S(1)}, u32[]{:S(2)}, u32[]{:S(2)}) %collective-permute-start.2) | collective-permute-done | bytes 16416 | tf_op jit(solution)/shard_map/ppermute | solution.py:19
  104.1 0.2 fusion.179
  104.3 2.4 %collective-permute-start.3 = (f32[1,1,32,128]{3,2,1,0:T(8,128)S(1)}, f32[1,1,32,128]{3,2,1,0:T(8,128)S(1)}, u32[]{:S(2)}, u32[]{:S(2)}) collective-permute-start(f32[1,1,32,128]{3,2,1,0:T(8,128)S(1)} %get-tuple-element.50), channel_id=1, source_target_pairs={{1,0},{2,1},{3,2},{5,4},{6,5},{7,6},{9,8},{10,9},{11,10},{13,12},{... | collective-permute-start | bytes 49160 | tf_op jit(solution)/shard_map/ppermute | solution.py:21
  106.8 1.3 collective-permute-start.4
  108.2 4.2 %collective-permute-done.4 = f32[1,1,32,128]{3,2,1,0:T(8,128)S(1)} collective-permute-done((f32[1,1,32,128]{3,2,1,0:T(8,128)S(1)}, f32[1,1,32,128]{3,2,1,0:T(8,128)S(1)}, u32[]{:S(2)}, u32[]{:S(2)}) %collective-permute-start.4) | collective-permute-done | bytes 16416 | tf_op jit(solution)/shard_map/ppermute | solution.py:19
  112.4 0.2 fusion.167
  112.7 2.4 %collective-permute-start.5 = (f32[1,1,32,128]{3,2,1,0:T(8,128)S(1)}, f32[1,1,32,128]{3,2,1,0:T(8,128)S(1)}, u32[]{:S(2)}, u32[]{:S(2)}) collective-permute-start(f32[1,1,32,128]{3,2,1,0:T(8,128)S(1)} %get-tuple-element.44), channel_id=1, source_target_pairs={{1,0},{2,1},{3,2},{5,4},{6,5},{7,6},{9,8},{10,9},{11,10},{13,12},{... | collective-permute-start | bytes 49160 | tf_op jit(solution)/shard_map/ppermute | solution.py:21
  115.1 1.3 collective-permute-start.6
  116.5 4.2 %collective-permute-done.6 = f32[1,1,32,128]{3,2,1,0:T(8,128)S(1)} collective-permute-done((f32[1,1,32,128]{3,2,1,0:T(8,128)S(1)}, f32[1,1,32,128]{3,2,1,0:T(8,128)S(1)}, u32[]{:S(2)}, u32[]{:S(2)}) %collective-permute-start.6) | collective-permute-done | bytes 16416 | tf_op jit(solution)/shard_map/ppermute | solution.py:19
  120.7 0.2 fusion.155
  121.0 1.9 collective-permute-start.7
  122.9 1.3 collective-permute-start.8
  124.4 4.2 %collective-permute-done.8 = f32[1,1,32,128]{3,2,1,0:T(8,128)S(1)} collective-permute-done((f32[1,1,32,128]{3,2,1,0:T(8,128)S(1)}, f32[1,1,32,128]{3,2,1,0:T(8,128)S(1)}, u32[]{:S(2)}, u32[]{:S(2)}) %collective-permute-start.8) | collective-permute-done | bytes 16416 | tf_op jit(solution)/shard_map/ppermute | solution.py:19
  128.6 0.2 fusion.143
  129.0 1.9 collective-permute-start.11
  130.9 1.3 collective-permute-start.12
  132.2 1.3 collective-permute-start.10
  133.5 5.2 %collective-permute-start.9 = (f32[1,1,32,128]{3,2,1,0:T(8,128)S(1)}, f32[1,1,32,128]{3,2,1,0:T(8,128)S(1)}, u32[]{:S(2)}, u32[]{:S(2)}) collective-permute-start(f32[1,1,32,128]{3,2,1,0:T(8,128)S(1)} %get-tuple-element.32), channel_id=1, source_target_pairs={{1,0},{2,1},{3,2},{5,4},{6,5},{7,6},{9,8},{10,9},{11,10},{13,12},{... | collective-permute-start | bytes 49160 | tf_op jit(solution)/shard_map/ppermute | solution.py:21
  138.7 0.2 fusion.119
  139.1 1.0 collective-permute-done.9
  140.1 0.2 fusion.131
  140.5 4.2 %collective-permute-start.13 = (f32[1,1,32,128]{3,2,1,0:T(8,128)S(1)}, f32[1,1,32,128]{3,2,1,0:T(8,128)S(1)}, u32[]{:S(2)}, u32[]{:S(2)}) collective-permute-start(f32[1,1,32,128]{3,2,1,0:T(8,128)S(1)} %get-tuple-element.80), channel_id=1, source_target_pairs={{1,0},{2,1},{3,2},{5,4},{6,5},{7,6},{9,8},{10,9},{11,10},{13,12},{... | collective-permute-start | bytes 49160 | tf_op jit(solution)/shard_map/ppermute | solution.py:21
  144.7 1.3 collective-permute-start.14
  146.0 4.6 %collective-permute-start.21 = (f32[1,1,32,128]{3,2,1,0:T(8,128)S(1)}, f32[1,1,32,128]{3,2,1,0:T(8,128)S(1)}, u32[]{:S(2)}, u32[]{:S(2)}) collective-permute-start(f32[1,1,32,128]{3,2,1,0:T(8,128)S(1)} %get-tuple-element.116), channel_id=1, source_target_pairs={{1,0},{2,1},{3,2},{5,4},{6,5},{7,6},{9,8},{10,9},{11,10},{13,12},{... | collective-permute-start | bytes 49160 | tf_op jit(solution)/shard_map/ppermute | solution.py:21
  150.6 1.3 collective-permute-start.22
  151.9 0.2 fusion.107
  152.2 4.1 %collective-permute-done.22 = f32[1,1,32,128]{3,2,1,0:T(8,128)S(1)} collective-permute-done((f32[1,1,32,128]{3,2,1,0:T(8,128)S(1)}, f32[1,1,32,128]{3,2,1,0:T(8,128)S(1)}, u32[]{:S(2)}, u32[]{:S(2)}) %collective-permute-start.22) | collective-permute-done | bytes 16416 | tf_op jit(solution)/shard_map/ppermute | solution.py:19
  156.3 0.2 fusion.59
  156.7 3.8 %collective-permute-start.15 = (f32[1,1,32,128]{3,2,1,0:T(8,128)S(1)}, f32[1,1,32,128]{3,2,1,0:T(8,128)S(1)}, u32[]{:S(2)}, u32[]{:S(2)}) collective-permute-start(f32[1,1,32,128]{3,2,1,0:T(8,128)S(1)} %get-tuple-element.74), channel_id=1, source_target_pairs={{1,0},{2,1},{3,2},{5,4},{6,5},{7,6},{9,8},{10,9},{11,10},{13,12},{... | collective-permute-start | bytes 49160 | tf_op jit(solution)/shard_map/ppermute | solution.py:21
  160.5 1.3 collective-permute-start.16
  161.8 4.5 %collective-permute-start.23 = (f32[1,1,32,128]{3,2,1,0:T(8,128)S(1)}, f32[1,1,32,128]{3,2,1,0:T(8,128)S(1)}, u32[]{:S(2)}, u32[]{:S(2)}) collective-permute-start(f32[1,1,32,128]{3,2,1,0:T(8,128)S(1)} %get-tuple-element.110), channel_id=1, source_target_pairs={{1,0},{2,1},{3,2},{5,4},{6,5},{7,6},{9,8},{10,9},{11,10},{13,12},{... | collective-permute-start | bytes 49160 | tf_op jit(solution)/shard_map/ppermute | solution.py:21
  166.3 1.3 collective-permute-start.24
  167.6 0.2 fusion.95
  168.0 3.9 %collective-permute-done.24 = f32[1,1,32,128]{3,2,1,0:T(8,128)S(1)} collective-permute-done((f32[1,1,32,128]{3,2,1,0:T(8,128)S(1)}, f32[1,1,32,128]{3,2,1,0:T(8,128)S(1)}, u32[]{:S(2)}, u32[]{:S(2)}) %collective-permute-start.24) | collective-permute-done | bytes 16416 | tf_op jit(solution)/shard_map/ppermute | solution.py:19
  172.3 1.9 collective-permute-start.17
  174.2 1.3 collective-permute-start.18
  175.5 4.5 %collective-permute-start.25 = (f32[1,1,32,128]{3,2,1,0:T(8,128)S(1)}, f32[1,1,32,128]{3,2,1,0:T(8,128)S(1)}, u32[]{:S(2)}, u32[]{:S(2)}) collective-permute-start(f32[1,1,32,128]{3,2,1,0:T(8,128)S(1)} %get-tuple-element.104), channel_id=1, source_target_pairs={{1,0},{2,1},{3,2},{5,4},{6,5},{7,6},{9,8},{10,9},{11,10},{13,12},{... | collective-permute-start | bytes 49160 | tf_op jit(solution)/shard_map/ppermute | solution.py:21
  180.1 1.3 collective-permute-start.26
  181.4 0.2 fusion.83
  181.8 4.1 %collective-permute-done.26 = f32[1,1,32,128]{3,2,1,0:T(8,128)S(1)} collective-permute-done((f32[1,1,32,128]{3,2,1,0:T(8,128)S(1)}, f32[1,1,32,128]{3,2,1,0:T(8,128)S(1)}, u32[]{:S(2)}, u32[]{:S(2)}) %collective-permute-start.26) | collective-permute-done | bytes 16416 | tf_op jit(solution)/shard_map/ppermute | solution.py:19
  186.2 1.8 collective-permute-start.27
  188.0 1.3 collective-permute-start.28
  189.3 4.5 %collective-permute-start.19 = (f32[1,1,32,128]{3,2,1,0:T(8,128)S(1)}, f32[1,1,32,128]{3,2,1,0:T(8,128)S(1)}, u32[]{:S(2)}, u32[]{:S(2)}) collective-permute-start(f32[1,1,32,128]{3,2,1,0:T(8,128)S(1)} %get-tuple-element.62), channel_id=1, source_target_pairs={{1,0},{2,1},{3,2},{5,4},{6,5},{7,6},{9,8},{10,9},{11,10},{13,12},{... | collective-permute-start | bytes 49160 | tf_op jit(solution)/shard_map/ppermute | solution.py:21
  193.9 1.3 collective-permute-start.20
  195.2 0.2 fusion.23
  195.5 4.5 %collective-permute-start.29 = (f32[1,1,32,128]{3,2,1,0:T(8,128)S(1)}, f32[1,1,32,128]{3,2,1,0:T(8,128)S(1)}, u32[]{:S(2)}, u32[]{:S(2)}) collective-permute-start(f32[1,1,32,128]{3,2,1,0:T(8,128)S(1)} %get-tuple-element.92), channel_id=1, source_target_pairs={{1,0},{2,1},{3,2},{5,4},{6,5},{7,6},{9,8},{10,9},{11,10},{13,12},{... | collective-permute-start | bytes 49160 | tf_op jit(solution)/shard_map/ppermute | solution.py:21
  200.0 1.3 collective-permute-start.30
  201.3 0.2 fusion.71
  201.7 4.0 %collective-permute-done.30 = f32[1,1,32,128]{3,2,1,0:T(8,128)S(1)} collective-permute-done((f32[1,1,32,128]{3,2,1,0:T(8,128)S(1)}, f32[1,1,32,128]{3,2,1,0:T(8,128)S(1)}, u32[]{:S(2)}, u32[]{:S(2)}) %collective-permute-start.30) | collective-permute-done | bytes 16416 | tf_op jit(solution)/shard_map/ppermute | solution.py:19
  205.9 0.7 fusion
  (80 shorter events, 2.8 us)
Async XLA Ops:
  6.5 36.2 %all-gather.4.cloned.1.call-start = ((), (), s32[]{:S(2)}) async-start(), calls=%async_computation | async-start | bytes 1179648 | tf_op jit(solution)/shard_map/all_gather | solution.py:30
  18.1 1.5 copy-start
  18.1 50.0 %all-gather.6.cloned.1.call-start = ((), (), s32[]{:S(2)}) async-start(), calls=%async_computation.1 | async-start | bytes 1179648 | tf_op jit(solution)/shard_map/all_gather | solution.py:30
  18.9 74.7 %all-gather.8.cloned.1.call-start = ((), (), s32[]{:S(2)}) async-start(), calls=%async_computation.2 | async-start | bytes 1179648 | tf_op jit(solution)/shard_map/all_gather | solution.py:30
  19.7 75.3 %collective-permute-start = (f32[1,32,128]{2,1,0:T(8,128)S(1)}, f32[1,32,128]{2,1,0:T(8,128)S(1)}, u32[]{:S(2)}, u32[]{:S(2)}) collective-permute-start(f32[1,32,128]{2,1,0:T(8,128)S(1)} %slice_bitcast_fusion.1), channel_id=1, source_target_pairs={{0,1},{1,2},{2,3},{4,5},{5,6},{6,7},{8,9},{9,10},{10,11},{12,13},{... | collective-permute-start | bytes 49160 | tf_op jit(solution)/shard_map/ppermute | solution.py:36
  94.9 0.9 copy-start.1
  96.0 3.9 %collective-permute-start.1 = (f32[1,1,32,128]{3,2,1,0:T(8,128)S(1)}, f32[1,1,32,128]{3,2,1,0:T(8,128)S(1)}, u32[]{:S(2)}, u32[]{:S(2)}) collective-permute-start(f32[1,1,32,128]{3,2,1,0:T(8,128)S(1)} %get-tuple-element.56), channel_id=1, source_target_pairs={{1,0},{2,1},{3,2},{5,4},{6,5},{7,6},{9,8},{10,9},{11,10},{13,12},{... | collective-permute-start | bytes 49160 | tf_op jit(solution)/shard_map/ppermute | solution.py:21
  98.4 5.6 %collective-permute-start.2 = (f32[1,1,32,128]{3,2,1,0:T(8,128)S(1)}, f32[1,1,32,128]{3,2,1,0:T(8,128)S(1)}, u32[]{:S(2)}, u32[]{:S(2)}) collective-permute-start(f32[1,1,32,128]{3,2,1,0:T(8,128)S(1)} %get-tuple-element.57), channel_id=1, source_target_pairs={{0,1},{1,2},{2,3},{4,5},{5,6},{6,7},{8,9},{9,10},{10,11},{12,13},{... | collective-permute-start | bytes 49160 | tf_op jit(solution)/shard_map/ppermute | solution.py:19
  104.3 3.9 %collective-permute-start.3 = (f32[1,1,32,128]{3,2,1,0:T(8,128)S(1)}, f32[1,1,32,128]{3,2,1,0:T(8,128)S(1)}, u32[]{:S(2)}, u32[]{:S(2)}) collective-permute-start(f32[1,1,32,128]{3,2,1,0:T(8,128)S(1)} %get-tuple-element.50), channel_id=1, source_target_pairs={{1,0},{2,1},{3,2},{5,4},{6,5},{7,6},{9,8},{10,9},{11,10},{13,12},{... | collective-permute-start | bytes 49160 | tf_op jit(solution)/shard_map/ppermute | solution.py:21
  106.8 5.6 %collective-permute-start.4 = (f32[1,1,32,128]{3,2,1,0:T(8,128)S(1)}, f32[1,1,32,128]{3,2,1,0:T(8,128)S(1)}, u32[]{:S(2)}, u32[]{:S(2)}) collective-permute-start(f32[1,1,32,128]{3,2,1,0:T(8,128)S(1)} %get-tuple-element.51), channel_id=1, source_target_pairs={{0,1},{1,2},{2,3},{4,5},{5,6},{6,7},{8,9},{9,10},{10,11},{12,13},{... | collective-permute-start | bytes 49160 | tf_op jit(solution)/shard_map/ppermute | solution.py:19
  112.7 3.9 %collective-permute-start.5 = (f32[1,1,32,128]{3,2,1,0:T(8,128)S(1)}, f32[1,1,32,128]{3,2,1,0:T(8,128)S(1)}, u32[]{:S(2)}, u32[]{:S(2)}) collective-permute-start(f32[1,1,32,128]{3,2,1,0:T(8,128)S(1)} %get-tuple-element.44), channel_id=1, source_target_pairs={{1,0},{2,1},{3,2},{5,4},{6,5},{7,6},{9,8},{10,9},{11,10},{13,12},{... | collective-permute-start | bytes 49160 | tf_op jit(solution)/shard_map/ppermute | solution.py:21
  115.1 5.6 %collective-permute-start.6 = (f32[1,1,32,128]{3,2,1,0:T(8,128)S(1)}, f32[1,1,32,128]{3,2,1,0:T(8,128)S(1)}, u32[]{:S(2)}, u32[]{:S(2)}) collective-permute-start(f32[1,1,32,128]{3,2,1,0:T(8,128)S(1)} %get-tuple-element.45), channel_id=1, source_target_pairs={{0,1},{1,2},{2,3},{4,5},{5,6},{6,7},{8,9},{9,10},{10,11},{12,13},{... | collective-permute-start | bytes 49160 | tf_op jit(solution)/shard_map/ppermute | solution.py:19
  121.0 3.4 %collective-permute-start.7 = (f32[1,1,32,128]{3,2,1,0:T(8,128)S(1)}, f32[1,1,32,128]{3,2,1,0:T(8,128)S(1)}, u32[]{:S(2)}, u32[]{:S(2)}) collective-permute-start(f32[1,1,32,128]{3,2,1,0:T(8,128)S(1)} %get-tuple-element.38), channel_id=1, source_target_pairs={{1,0},{2,1},{3,2},{5,4},{6,5},{7,6},{9,8},{10,9},{11,10},{13,12},{... | collective-permute-start | bytes 49160 | tf_op jit(solution)/shard_map/ppermute | solution.py:21
  122.9 5.6 %collective-permute-start.8 = (f32[1,1,32,128]{3,2,1,0:T(8,128)S(1)}, f32[1,1,32,128]{3,2,1,0:T(8,128)S(1)}, u32[]{:S(2)}, u32[]{:S(2)}) collective-permute-start(f32[1,1,32,128]{3,2,1,0:T(8,128)S(1)} %get-tuple-element.39), channel_id=1, source_target_pairs={{0,1},{1,2},{2,3},{4,5},{5,6},{6,7},{8,9},{9,10},{10,11},{12,13},{... | collective-permute-start | bytes 49160 | tf_op jit(solution)/shard_map/ppermute | solution.py:19
  129.0 9.7 %collective-permute-start.11 = (f32[1,1,32,128]{3,2,1,0:T(8,128)S(1)}, f32[1,1,32,128]{3,2,1,0:T(8,128)S(1)}, u32[]{:S(2)}, u32[]{:S(2)}) collective-permute-start(f32[1,1,32,128]{3,2,1,0:T(8,128)S(1)} %get-tuple-element.86), channel_id=1, source_target_pairs={{1,0},{2,1},{3,2},{5,4},{6,5},{7,6},{9,8},{10,9},{11,10},{13,12},{... | collective-permute-start | bytes 49160 | tf_op jit(solution)/shard_map/ppermute | solution.py:21
  130.9 7.8 %collective-permute-start.12 = (f32[1,1,32,128]{3,2,1,0:T(8,128)S(1)}, f32[1,1,32,128]{3,2,1,0:T(8,128)S(1)}, u32[]{:S(2)}, u32[]{:S(2)}) collective-permute-start(f32[1,1,32,128]{3,2,1,0:T(8,128)S(1)} %get-tuple-element.87), channel_id=1, source_target_pairs={{0,1},{1,2},{2,3},{4,5},{5,6},{6,7},{8,9},{9,10},{10,11},{12,13},{... | collective-permute-start | bytes 49160 | tf_op jit(solution)/shard_map/ppermute | solution.py:19
  132.2 6.9 %collective-permute-start.10 = (f32[1,1,32,128]{3,2,1,0:T(8,128)S(1)}, f32[1,1,32,128]{3,2,1,0:T(8,128)S(1)}, u32[]{:S(2)}, u32[]{:S(2)}) collective-permute-start(f32[1,1,32,128]{3,2,1,0:T(8,128)S(1)} %get-tuple-element.33), channel_id=1, source_target_pairs={{0,1},{1,2},{2,3},{4,5},{5,6},{6,7},{8,9},{9,10},{10,11},{12,13},{... | collective-permute-start | bytes 49160 | tf_op jit(solution)/shard_map/ppermute | solution.py:19
  133.5 6.6 %collective-permute-start.9 = (f32[1,1,32,128]{3,2,1,0:T(8,128)S(1)}, f32[1,1,32,128]{3,2,1,0:T(8,128)S(1)}, u32[]{:S(2)}, u32[]{:S(2)}) collective-permute-start(f32[1,1,32,128]{3,2,1,0:T(8,128)S(1)} %get-tuple-element.32), channel_id=1, source_target_pairs={{1,0},{2,1},{3,2},{5,4},{6,5},{7,6},{9,8},{10,9},{11,10},{13,12},{... | collective-permute-start | bytes 49160 | tf_op jit(solution)/shard_map/ppermute | solution.py:21
  140.5 11.4 %collective-permute-start.13 = (f32[1,1,32,128]{3,2,1,0:T(8,128)S(1)}, f32[1,1,32,128]{3,2,1,0:T(8,128)S(1)}, u32[]{:S(2)}, u32[]{:S(2)}) collective-permute-start(f32[1,1,32,128]{3,2,1,0:T(8,128)S(1)} %get-tuple-element.80), channel_id=1, source_target_pairs={{1,0},{2,1},{3,2},{5,4},{6,5},{7,6},{9,8},{10,9},{11,10},{13,12},{... | collective-permute-start | bytes 49160 | tf_op jit(solution)/shard_map/ppermute | solution.py:21
  144.7 7.2 %collective-permute-start.14 = (f32[1,1,32,128]{3,2,1,0:T(8,128)S(1)}, f32[1,1,32,128]{3,2,1,0:T(8,128)S(1)}, u32[]{:S(2)}, u32[]{:S(2)}) collective-permute-start(f32[1,1,32,128]{3,2,1,0:T(8,128)S(1)} %get-tuple-element.81), channel_id=1, source_target_pairs={{0,1},{1,2},{2,3},{4,5},{5,6},{6,7},{8,9},{9,10},{10,11},{12,13},{... | collective-permute-start | bytes 49160 | tf_op jit(solution)/shard_map/ppermute | solution.py:19
  146.0 6.2 %collective-permute-start.21 = (f32[1,1,32,128]{3,2,1,0:T(8,128)S(1)}, f32[1,1,32,128]{3,2,1,0:T(8,128)S(1)}, u32[]{:S(2)}, u32[]{:S(2)}) collective-permute-start(f32[1,1,32,128]{3,2,1,0:T(8,128)S(1)} %get-tuple-element.116), channel_id=1, source_target_pairs={{1,0},{2,1},{3,2},{5,4},{6,5},{7,6},{9,8},{10,9},{11,10},{13,12},{... | collective-permute-start | bytes 49160 | tf_op jit(solution)/shard_map/ppermute | solution.py:21
  150.6 5.8 %collective-permute-start.22 = (f32[1,1,32,128]{3,2,1,0:T(8,128)S(1)}, f32[1,1,32,128]{3,2,1,0:T(8,128)S(1)}, u32[]{:S(2)}, u32[]{:S(2)}) collective-permute-start(f32[1,1,32,128]{3,2,1,0:T(8,128)S(1)} %get-tuple-element.117), channel_id=1, source_target_pairs={{0,1},{1,2},{2,3},{4,5},{5,6},{6,7},{8,9},{9,10},{10,11},{12,13},{... | collective-permute-start | bytes 49160 | tf_op jit(solution)/shard_map/ppermute | solution.py:19
  156.7 11.0 %collective-permute-start.15 = (f32[1,1,32,128]{3,2,1,0:T(8,128)S(1)}, f32[1,1,32,128]{3,2,1,0:T(8,128)S(1)}, u32[]{:S(2)}, u32[]{:S(2)}) collective-permute-start(f32[1,1,32,128]{3,2,1,0:T(8,128)S(1)} %get-tuple-element.74), channel_id=1, source_target_pairs={{1,0},{2,1},{3,2},{5,4},{6,5},{7,6},{9,8},{10,9},{11,10},{13,12},{... | collective-permute-start | bytes 49160 | tf_op jit(solution)/shard_map/ppermute | solution.py:21
  160.5 7.2 %collective-permute-start.16 = (f32[1,1,32,128]{3,2,1,0:T(8,128)S(1)}, f32[1,1,32,128]{3,2,1,0:T(8,128)S(1)}, u32[]{:S(2)}, u32[]{:S(2)}) collective-permute-start(f32[1,1,32,128]{3,2,1,0:T(8,128)S(1)} %get-tuple-element.75), channel_id=1, source_target_pairs={{0,1},{1,2},{2,3},{4,5},{5,6},{6,7},{8,9},{9,10},{10,11},{12,13},{... | collective-permute-start | bytes 49160 | tf_op jit(solution)/shard_map/ppermute | solution.py:19
  161.8 6.2 %collective-permute-start.23 = (f32[1,1,32,128]{3,2,1,0:T(8,128)S(1)}, f32[1,1,32,128]{3,2,1,0:T(8,128)S(1)}, u32[]{:S(2)}, u32[]{:S(2)}) collective-permute-start(f32[1,1,32,128]{3,2,1,0:T(8,128)S(1)} %get-tuple-element.110), channel_id=1, source_target_pairs={{1,0},{2,1},{3,2},{5,4},{6,5},{7,6},{9,8},{10,9},{11,10},{13,12},{... | collective-permute-start | bytes 49160 | tf_op jit(solution)/shard_map/ppermute | solution.py:21
  166.3 5.6 %collective-permute-start.24 = (f32[1,1,32,128]{3,2,1,0:T(8,128)S(1)}, f32[1,1,32,128]{3,2,1,0:T(8,128)S(1)}, u32[]{:S(2)}, u32[]{:S(2)}) collective-permute-start(f32[1,1,32,128]{3,2,1,0:T(8,128)S(1)} %get-tuple-element.111), channel_id=1, source_target_pairs={{0,1},{1,2},{2,3},{4,5},{5,6},{6,7},{8,9},{9,10},{10,11},{12,13},{... | collective-permute-start | bytes 49160 | tf_op jit(solution)/shard_map/ppermute | solution.py:19
  172.3 9.1 %collective-permute-start.17 = (f32[1,1,32,128]{3,2,1,0:T(8,128)S(1)}, f32[1,1,32,128]{3,2,1,0:T(8,128)S(1)}, u32[]{:S(2)}, u32[]{:S(2)}) collective-permute-start(f32[1,1,32,128]{3,2,1,0:T(8,128)S(1)} %get-tuple-element.68), channel_id=1, source_target_pairs={{1,0},{2,1},{3,2},{5,4},{6,5},{7,6},{9,8},{10,9},{11,10},{13,12},{... | collective-permute-start | bytes 49160 | tf_op jit(solution)/shard_map/ppermute | solution.py:21
  174.2 7.2 %collective-permute-start.18 = (f32[1,1,32,128]{3,2,1,0:T(8,128)S(1)}, f32[1,1,32,128]{3,2,1,0:T(8,128)S(1)}, u32[]{:S(2)}, u32[]{:S(2)}) collective-permute-start(f32[1,1,32,128]{3,2,1,0:T(8,128)S(1)} %get-tuple-element.69), channel_id=1, source_target_pairs={{0,1},{1,2},{2,3},{4,5},{5,6},{6,7},{8,9},{9,10},{10,11},{12,13},{... | collective-permute-start | bytes 49160 | tf_op jit(solution)/shard_map/ppermute | solution.py:19
  175.5 6.2 %collective-permute-start.25 = (f32[1,1,32,128]{3,2,1,0:T(8,128)S(1)}, f32[1,1,32,128]{3,2,1,0:T(8,128)S(1)}, u32[]{:S(2)}, u32[]{:S(2)}) collective-permute-start(f32[1,1,32,128]{3,2,1,0:T(8,128)S(1)} %get-tuple-element.104), channel_id=1, source_target_pairs={{1,0},{2,1},{3,2},{5,4},{6,5},{7,6},{9,8},{10,9},{11,10},{13,12},{... | collective-permute-start | bytes 49160 | tf_op jit(solution)/shard_map/ppermute | solution.py:21
  180.1 5.7 %collective-permute-start.26 = (f32[1,1,32,128]{3,2,1,0:T(8,128)S(1)}, f32[1,1,32,128]{3,2,1,0:T(8,128)S(1)}, u32[]{:S(2)}, u32[]{:S(2)}) collective-permute-start(f32[1,1,32,128]{3,2,1,0:T(8,128)S(1)} %get-tuple-element.105), channel_id=1, source_target_pairs={{0,1},{1,2},{2,3},{4,5},{5,6},{6,7},{8,9},{9,10},{10,11},{12,13},{... | collective-permute-start | bytes 49160 | tf_op jit(solution)/shard_map/ppermute | solution.py:19
  186.2 9.0 %collective-permute-start.27 = (f32[1,1,32,128]{3,2,1,0:T(8,128)S(1)}, f32[1,1,32,128]{3,2,1,0:T(8,128)S(1)}, u32[]{:S(2)}, u32[]{:S(2)}) collective-permute-start(f32[1,1,32,128]{3,2,1,0:T(8,128)S(1)} %get-tuple-element.98), channel_id=1, source_target_pairs={{1,0},{2,1},{3,2},{5,4},{6,5},{7,6},{9,8},{10,9},{11,10},{13,12},{... | collective-permute-start | bytes 49160 | tf_op jit(solution)/shard_map/ppermute | solution.py:21
  188.0 7.2 %collective-permute-start.28 = (f32[1,1,32,128]{3,2,1,0:T(8,128)S(1)}, f32[1,1,32,128]{3,2,1,0:T(8,128)S(1)}, u32[]{:S(2)}, u32[]{:S(2)}) collective-permute-start(f32[1,1,32,128]{3,2,1,0:T(8,128)S(1)} %get-tuple-element.99), channel_id=1, source_target_pairs={{0,1},{1,2},{2,3},{4,5},{5,6},{6,7},{8,9},{9,10},{10,11},{12,13},{... | collective-permute-start | bytes 49160 | tf_op jit(solution)/shard_map/ppermute | solution.py:19
  189.3 12.0 %collective-permute-start.19 = (f32[1,1,32,128]{3,2,1,0:T(8,128)S(1)}, f32[1,1,32,128]{3,2,1,0:T(8,128)S(1)}, u32[]{:S(2)}, u32[]{:S(2)}) collective-permute-start(f32[1,1,32,128]{3,2,1,0:T(8,128)S(1)} %get-tuple-element.62), channel_id=1, source_target_pairs={{1,0},{2,1},{3,2},{5,4},{6,5},{7,6},{9,8},{10,9},{11,10},{13,12},{... | collective-permute-start | bytes 49160 | tf_op jit(solution)/shard_map/ppermute | solution.py:21
  193.9 7.5 %collective-permute-start.20 = (f32[1,1,32,128]{3,2,1,0:T(8,128)S(1)}, f32[1,1,32,128]{3,2,1,0:T(8,128)S(1)}, u32[]{:S(2)}, u32[]{:S(2)}) collective-permute-start(f32[1,1,32,128]{3,2,1,0:T(8,128)S(1)} %get-tuple-element.63), channel_id=1, source_target_pairs={{0,1},{1,2},{2,3},{4,5},{5,6},{6,7},{8,9},{9,10},{10,11},{12,13},{... | collective-permute-start | bytes 49160 | tf_op jit(solution)/shard_map/ppermute | solution.py:19
  195.5 6.2 %collective-permute-start.29 = (f32[1,1,32,128]{3,2,1,0:T(8,128)S(1)}, f32[1,1,32,128]{3,2,1,0:T(8,128)S(1)}, u32[]{:S(2)}, u32[]{:S(2)}) collective-permute-start(f32[1,1,32,128]{3,2,1,0:T(8,128)S(1)} %get-tuple-element.92), channel_id=1, source_target_pairs={{1,0},{2,1},{3,2},{5,4},{6,5},{7,6},{9,8},{10,9},{11,10},{13,12},{... | collective-permute-start | bytes 49160 | tf_op jit(solution)/shard_map/ppermute | solution.py:21
  200.0 5.6 %collective-permute-start.30 = (f32[1,1,32,128]{3,2,1,0:T(8,128)S(1)}, f32[1,1,32,128]{3,2,1,0:T(8,128)S(1)}, u32[]{:S(2)}, u32[]{:S(2)}) collective-permute-start(f32[1,1,32,128]{3,2,1,0:T(8,128)S(1)} %get-tuple-element.93), channel_id=1, source_target_pairs={{0,1},{1,2},{2,3},{4,5},{5,6},{6,7},{8,9},{9,10},{10,11},{12,13},{... | collective-permute-start | bytes 49160 | tf_op jit(solution)/shard_map/ppermute | solution.py:19
Sparse Core Ops, SparseCore 0:
  18.3 24.4 all-gather.3
  44.7 23.4 all-gather.5
  70.1 23.4 all-gather.7
